TPU v7x, 256 devices: a whole 4x4x8 slice. The times are simulated.
256 devices in a mesh: segment: 8 (over x, core), seq: 32 (over z, y).
Axes of the slice: x: 4, y: 4, z: 8, core: 2. Of those that a mesh axis runs over, the one named last changes fastest.
Arguments:
- latent: bfloat16 [12288, 1536], P('seq'), may hold values from -4 to 4
- stale_kv: bfloat16 [8, 2, 12288, 1536], P('segment', None, 'seq'), may hold values from -3 to 3
- query_weight: bfloat16 [8, 1536, 1536], P('segment', 'seq'), may hold values from -0.15625 to 0.15625
- key_weight: bfloat16 [8, 1536, 1536], P('segment', 'seq'), may hold values from -0.15625 to 0.15625
- value_weight: bfloat16 [8, 1536, 1536], P('segment', 'seq'), may hold values from -0.15625 to 0.15625
- out_weight: bfloat16 [8, 1536, 1536], P('segment', 'seq'), may hold values from -0.3125 to 0.3125
- query_gain: float32 [8, 128], P('segment'), may hold values from 0.5 to 2
- key_gain: float32 [8, 128], P('segment'), may hold values from 0.5 to 2
- tile_mask: int32 [192, 6], P('seq'), may hold values from -1 to 191, as said below
Outputs:
- section_out: bfloat16 [8, 12288, 1536], P('segment', 'seq')
Inputs may be any that keep to these rules, and one draw needn't show every extreme that they name: `tile_mask`: row g lists the key tiles of query tile g: slot 0 holds g itself, the next slots distinct other tiles whose tile-frame (tile number // 6) differs from that of g by at most one, and the remaining slots -1. Every row lists two or more tiles, and some row lists 6.
All inputs are finite; a program needn't handle non-finite values.
Results may differ from a plain program's by a relative error of at most 0.027.
Values may be sent and summed in bfloat16 or wider, within the bound.
No kernel may reach another device: no remote copies, remote signals or barrier semaphores. Data moves between devices by JAX's collectives and lax.ppermute only.
A program may use at most 128 MiB of HBM per device.

v0:
```python
import math

import jax
import jax.numpy as jnp
from jax import lax
from jax.sharding import PartitionSpec as P

D = 1536
HEADS = 12
HEAD = 128
TILE = 64
PATCHES = 3
TPP = 2


epsilon = 1e-06


def extended(cells, sides, width):
    for axis, dim in sides:
        count = lax.axis_size(axis)
        ends = count - 1
        head = lax.slice_in_dim(cells, 0, width, axis=dim)
        tail = lax.slice_in_dim(cells, cells.shape[dim] - width, cells.shape[dim], axis=dim)
        cells = jnp.concatenate(
            [
                lax.ppermute(tail, axis, [(i, (i + 1) % count) for i in range(ends)]),
                cells,
                lax.ppermute(head, axis, [((i + 1) % count, i) for i in range(ends)]),
            ],
            axis=dim,
        )
    return cells


def from_behind(value, axis, by):
    count = lax.axis_size(axis)
    pairs = [(i, i + by) for i in range(count) if 0 <= i + by < count]
    return lax.ppermute(value, axis, pairs)


def head_normed(projected, gain):
    n_rows = projected.shape[0]
    heads = projected.reshape(n_rows, HEADS, HEAD)
    scaled = heads * lax.rsqrt(jnp.mean(heads * heads, axis=-1, keepdims=True) + epsilon)
    return (scaled * gain).reshape(n_rows, D).astype(jnp.bfloat16)


def keys_values(inputs, weight_k, weight_v, gain_k):
    keys = head_normed(jnp.dot(inputs, weight_k, preferred_element_type=jnp.float32), gain_k)
    values = jnp.dot(inputs, weight_v, preferred_element_type=jnp.float32).astype(jnp.bfloat16)
    return jnp.stack([keys, values])


def attend(queries, blocks, tile_index, usable):
    n_query = tile_index.shape[0]
    key_heads = jnp.take(blocks[0], tile_index, axis=0).reshape(n_query, -1, HEADS, HEAD)
    value_heads = jnp.take(blocks[1], tile_index, axis=0).reshape(n_query, -1, HEADS, HEAD)
    query_heads = queries.reshape(n_query, -1, HEADS, HEAD)
    scores = jnp.einsum(
        "pthe,pkhe->phtk", query_heads, key_heads, preferred_element_type=jnp.float32
    ) / math.sqrt(HEAD)
    listed = jnp.repeat(usable, TILE, axis=1).astype(jnp.float32)
    weights = jnp.exp(scores) * listed[:, None, None, :]
    totals = jnp.sum(weights, axis=-1)
    summed = jnp.einsum(
        "phtk,pkhe->pthe",
        weights.astype(jnp.bfloat16),
        value_heads,
        preferred_element_type=jnp.float32,
    )
    return summed / jnp.swapaxes(totals, 1, 2)[..., None]


def per_device(
    latent,
    stale_kv,
    query_weight,
    key_weight,
    value_weight,
    out_weight,
    query_gain,
    key_gain,
    tile_mask,
):
    tok_dev = latent.shape[0]
    patch_rows = tok_dev // PATCHES
    tiles_dev = tile_mask.shape[0]
    segment_id = lax.axis_index("segment")
    frame_id = lax.axis_index("seq")
    rounds = PATCHES + lax.axis_size("segment") - 1
    full_q, full_k, full_v, full_out = (
        lax.all_gather(query_weight[0], "seq", axis=0, tiled=True),
        lax.all_gather(key_weight[0], "seq", axis=0, tiled=True),
        lax.all_gather(value_weight[0], "seq", axis=0, tiled=True),
        lax.all_gather(out_weight[0], "seq", axis=0, tiled=True),
    )
    gain_q = query_gain[0]
    gain_k = key_gain[0]
    local_kv = stale_kv[0]
    window = extended(local_kv, (("seq", 1),), tok_dev)
    zero_rows = jnp.zeros((patch_rows, D), jnp.bfloat16)
    zero_pair = jnp.zeros((2, patch_rows, D), jnp.bfloat16)

    def project(inputs):
        fresh_q = head_normed(jnp.dot(inputs, full_q, preferred_element_type=jnp.float32), gain_q)
        return (fresh_q, keys_values(inputs, full_k, full_v, gain_k))

    def skip_project(inputs):
        return (zero_rows, zero_pair)

    def advance(round_id, carry):
        window, received, result = carry
        patch_id = round_id - segment_id
        active = (patch_id >= 0) & (patch_id < PATCHES)
        current = jnp.clip(patch_id, 0, PATCHES - 1)
        offset = current * patch_rows
        entering = lax.dynamic_slice_in_dim(latent, offset, patch_rows, 0)
        inputs = jnp.where(segment_id == 0, entering, received)
        fresh_q, own_kv = lax.cond(active, project, skip_project, inputs)
        spread = extended(own_kv, (("seq", 1),), patch_rows)
        trailing = spread[:, :patch_rows]
        leading = spread[:, 2 * patch_rows :]

        def finish(state):
            former, stored = state
            updated = lax.dynamic_update_slice_in_dim(former, trailing, offset, 1)
            updated = lax.dynamic_update_slice_in_dim(updated, own_kv, tok_dev + offset, 1)
            updated = lax.dynamic_update_slice_in_dim(updated, leading, 2 * tok_dev + offset, 1)
            listing = lax.dynamic_slice_in_dim(tile_mask, current * TPP, TPP, 0)
            usable = listing >= 0
            tile_index = jnp.where(usable, listing - (frame_id - 1) * tiles_dev, 0)
            blocks = updated.reshape(2, 3 * tiles_dev, TILE, D)
            attention = attend(fresh_q.reshape(TPP, TILE, D), blocks, tile_index, usable)
            attention_b = attention.reshape(patch_rows, D).astype(jnp.bfloat16)
            mixed = jnp.dot(attention_b, full_out, preferred_element_type=jnp.float32)
            leaving = (inputs.astype(jnp.float32) + mixed).astype(jnp.bfloat16)
            stored = lax.dynamic_update_slice_in_dim(stored, leaving, offset, 0)
            return (updated, stored, leaving)

        def remain(state):
            return (state[0], state[1], zero_rows)

        window, result, leaving = lax.cond(active, finish, remain, (window, result))
        received = from_behind(leaving, "segment", 1)
        return (window, received, result)

    initial = (window, zero_rows, jnp.zeros((tok_dev, D), jnp.bfloat16))
    final_state = lax.fori_loop(0, rounds, advance, initial)
    return final_state[2][None]


def solution(mesh):
    return jax.shard_map(
        per_device,
        mesh=mesh,
        in_specs=(
            P("seq", None),
            P("segment", None, "seq", None),
            P("segment", "seq", None),
            P("segment", "seq", None),
            P("segment", "seq", None),
            P("segment", "seq", None),
            P("segment", None),
            P("segment", None),
            P("seq", None),
        ),
        out_specs=P("segment", "seq", None),
        check_vma=False,
    )
```

profile of v0, /device:TPU:111, one launch (start us, length us, event | category | flops | bytes accessed | tf_op | source)
XLA Modules:
  0.0 1287.4 jit_solution(12764874456746758375)
XLA Ops:
  14.6 54.2 %collective-permute-done.3 = bf16[2,384,1536]{2,1,0:T(8,128)(2,1)S(1)} collective-permute-done((bf16[2,384,1536]{2,1,0:T(8,128)(2,1)}, bf16[2,384,1536]{2,1,0:T(8,128)(2,1)S(1)}, u32[]{:S(2)}, u32[]{:S(2)}) %collective-permute-start.3) | collective-permute-done | bytes 2359328 | tf_op jit(solution)/shard_map/ppermute | solution.py:27
  68.9 4.8 collective-permute-done.4
  73.7 5.7 pad_maximum_fusion.1
  79.5 19.3 %all-gather.9.cloned.1.call-done = bf16[1,1536,1536]{2,1,0:T(8,128)(2,1)} async-done(((bf16[1,48,1536]{2,1,0:T(8,128)(2,1)}), bf16[1,1536,1536]{2,1,0:T(8,128)(2,1)}) %all-gather.9.cloned.1.call-update) | async-done | bytes 4718608 | tf_op jit(solution)/shard_map/all_gather | solution.py:93
  98.8 87.5 %all-gather.11.cloned.1.call-done = bf16[1,1536,1536]{2,1,0:T(8,128)(2,1)} async-done(((bf16[1,48,1536]{2,1,0:T(8,128)(2,1)}), bf16[1,1536,1536]{2,1,0:T(8,128)(2,1)}) %all-gather.11.cloned.1.call-update) | async-done | bytes 4718608 | tf_op jit(solution)/shard_map/all_gather | solution.py:94
  186.2 83.4 %all-gather.13.cloned.1.call-done = bf16[1,1536,1536]{2,1,0:T(8,128)(2,1)} async-done(((bf16[1,48,1536]{2,1,0:T(8,128)(2,1)}), bf16[1,1536,1536]{2,1,0:T(8,128)(2,1)}) %all-gather.13.cloned.1.call-update) | async-done | bytes 4718608 | tf_op jit(solution)/shard_map/all_gather | solution.py:95
  269.7 83.3 %all-gather.15.cloned.1.call-done = bf16[1,1536,1536]{2,1,0:T(8,128)(2,1)} async-done(((bf16[1,48,1536]{2,1,0:T(8,128)(2,1)}), bf16[1,1536,1536]{2,1,0:T(8,128)(2,1)}) %all-gather.15.cloned.1.call-update) | async-done | bytes 4718608 | tf_op jit(solution)/shard_map/all_gather | solution.py:96
  354.1 926.8 %while.18 = (s32[]{:T(128)}, bf16[2,1152,1536]{2,1,0:T(8,128)(2,1)}, bf16[128,1536]{1,0:T(8,128)(2,1)S(1)}, bf16[384,1536]{1,0:T(8,128)(2,1)}, s32[]{:T(128)}, /...) while((s32[]{:T(128)}, ...), condition=%wide.region_8.10_spmd, body=%wide.region_0.9_spmd.sunk | while | flops 2727545344 | bytes 147957200 | solution.py:149
  360.9 12.2 collective-permute-done
  377.6 6.7 collective-permute-done.2
  391.3 9.9 collective-permute-done
  401.3 5.9 collective-permute-done.1
  409.2 8.9 collective-permute-done.2
  424.7 8.6 collective-permute-done
  433.2 5.2 collective-permute-done.1
  440.5 10.0 collective-permute-done.2
  457.1 9.7 collective-permute-done
  466.7 5.2 collective-permute-done.1
  474.0 8.9 collective-permute-done.2
  489.5 9.7 collective-permute-done
  499.1 5.2 collective-permute-done.1
  506.5 8.9 collective-permute-done.2
  521.9 9.7 collective-permute-done
  531.5 5.2 collective-permute-done.1
  538.9 8.9 collective-permute-done.2
  554.3 7.4 collective-permute-done
  561.7 5.2 collective-permute-done.1
  569.1 419.4 %collective-permute-done.2 = bf16[128,1536]{1,0:T(8,128)(2,1)S(1)} collective-permute-done((bf16[128,1536]{1,0:T(8,128)(2,1)}, bf16[128,1536]{1,0:T(8,128)(2,1)S(1)}, u32[]{:S(2)}, u32[]{:S(2)}) %collective-permute-start.2) | collective-permute-done | bytes 393248 | tf_op jit(solution)/shard_map/while/body/eval_jaxpr/ppermute | solution.py:39
  989.6 9.9 conditional.4
  1005.1 7.2 collective-permute-done
  1012.2 5.5 collective-permute-done.1
  1017.8 54.0 %conditional.5 = (bf16[2,1152,1536]{2,1,0:T(8,128)(2,1)}, bf16[384,1536]{1,0:T(8,128)(2,1)}, bf16[128,1536]{1,0:T(8,128)(2,1)}) conditional(s32[]{:T(128)} %convert_element_type.58, (bf16[2,1152,1536]{2,1,0:T(8,128)(2,1)}, bf16[384,1536]{1,0:T(8,128)(2,1)}) %tuple.60, (s32[]{:T(128)}, bf16[2,1152,1536]{2,1,0:T(8,128)(2,1)}, ...), branch_computations={%region_5.5_spmd, %region_6.8_spmd} | conditional | flops 912850560 | bytes 86146920 | solution.py:144
  1017.8 4.6 dynamic_update_slice.8
  1022.4 4.5 dynamic_update_slice.9
  1026.9 4.5 dynamic_update_slice.10
  1031.4 5.3 fusion.25
  1038.7 4.2 gather_fusion
  1045.1 4.2 broadcast_select_fusion
  1049.3 5.5 reshape.55
  1055.2 4.7 bitcast_reduce_fusion
  1073.1 13.7 %collective-permute-done.2 = bf16[128,1536]{1,0:T(8,128)(2,1)S(1)} collective-permute-done((bf16[128,1536]{1,0:T(8,128)(2,1)}, bf16[128,1536]{1,0:T(8,128)(2,1)S(1)}, u32[]{:S(2)}, u32[]{:S(2)}) %collective-permute-start.2) | collective-permute-done | bytes 393248 | tf_op jit(solution)/shard_map/while/body/eval_jaxpr/ppermute | solution.py:39
  1087.9 9.9 conditional.4
  1103.4 7.2 collective-permute-done
  1110.5 5.3 collective-permute-done.1
  1115.8 54.0 %conditional.5 = (bf16[2,1152,1536]{2,1,0:T(8,128)(2,1)}, bf16[384,1536]{1,0:T(8,128)(2,1)}, bf16[128,1536]{1,0:T(8,128)(2,1)}) conditional(s32[]{:T(128)} %convert_element_type.58, (bf16[2,1152,1536]{2,1,0:T(8,128)(2,1)}, bf16[384,1536]{1,0:T(8,128)(2,1)}) %tuple.60, (s32[]{:T(128)}, bf16[2,1152,1536]{2,1,0:T(8,128)(2,1)}, ...), branch_computations={%region_5.5_spmd, %region_6.8_spmd} | conditional | flops 912850560 | bytes 86146920 | solution.py:144
  1115.8 4.6 dynamic_update_slice.8
  1120.4 4.5 dynamic_update_slice.9
  1124.9 4.5 dynamic_update_slice.10
  1129.4 5.3 fusion.25
  1143.1 4.2 broadcast_select_fusion
  1147.3 5.5 reshape.55
  1153.2 4.7 bitcast_reduce_fusion
  1171.1 18.1 %collective-permute-done.2 = bf16[128,1536]{1,0:T(8,128)(2,1)S(1)} collective-permute-done((bf16[128,1536]{1,0:T(8,128)(2,1)}, bf16[128,1536]{1,0:T(8,128)(2,1)S(1)}, u32[]{:S(2)}, u32[]{:S(2)}) %collective-permute-start.2) | collective-permute-done | bytes 393248 | tf_op jit(solution)/shard_map/while/body/eval_jaxpr/ppermute | solution.py:39
  1190.3 9.9 conditional.4
  1205.8 12.5 collective-permute-done
  1218.3 5.0 collective-permute-done.1
  1223.2 53.8 %conditional.5 = (bf16[2,1152,1536]{2,1,0:T(8,128)(2,1)}, bf16[384,1536]{1,0:T(8,128)(2,1)}, bf16[128,1536]{1,0:T(8,128)(2,1)}) conditional(s32[]{:T(128)} %convert_element_type.58, (bf16[2,1152,1536]{2,1,0:T(8,128)(2,1)}, bf16[384,1536]{1,0:T(8,128)(2,1)}) %tuple.60, (s32[]{:T(128)}, bf16[2,1152,1536]{2,1,0:T(8,128)(2,1)}, ...), branch_computations={%region_5.5_spmd, %region_6.8_spmd} | conditional | flops 912850560 | bytes 86146920 | solution.py:144
  1223.2 4.6 dynamic_update_slice.8
  1227.8 4.5 dynamic_update_slice.9
  1232.3 4.4 dynamic_update_slice.10
  1236.7 5.3 fusion.25
  1250.4 4.2 broadcast_select_fusion
  1254.6 5.5 reshape.55
  1260.6 4.7 bitcast_reduce_fusion
  (228 shorter events, 191.2 us)
Async XLA Ops:
  6.5 92.2 %all-gather.9.cloned.1.call-start = ((), (), s32[]{:S(2)}) async-start(), calls=%async_computation | async-start | bytes 4866048 | tf_op jit(solution)/shard_map/all_gather | solution.py:93
  7.3 179.0 %all-gather.11.cloned.1.call-start = ((), (), s32[]{:S(2)}) async-start(), calls=%async_computation.1 | async-start | bytes 4866048 | tf_op jit(solution)/shard_map/all_gather | solution.py:94
  8.0 261.7 %all-gather.13.cloned.1.call-start = ((), (), s32[]{:S(2)}) async-start(), calls=%async_computation.2 | async-start | bytes 4866048 | tf_op jit(solution)/shard_map/all_gather | solution.py:95
  8.7 344.2 %all-gather.15.cloned.1.call-start = ((), (), s32[]{:S(2)}) async-start(), calls=%async_computation.3 | async-start | bytes 4866048 | tf_op jit(solution)/shard_map/all_gather | solution.py:96
  9.3 59.6 %collective-permute-start.3 = (bf16[2,384,1536]{2,1,0:T(8,128)(2,1)}, bf16[2,384,1536]{2,1,0:T(8,128)(2,1)S(1)}, u32[]{:S(2)}, u32[]{:S(2)}) collective-permute-start(bf16[2,384,1536]{2,1,0:T(8,128)(2,1)} %bitcast.66), channel_id=1, source_target_pairs={{0,1},{1,2},{2,3},{3,4},{4,5},{5,6},{6,7},{7,8},{8,9},{9,10},{10,1... | collective-permute-start | bytes 7077896 | tf_op jit(solution)/shard_map/ppermute | solution.py:27
  12.5 61.2 %collective-permute-start.4 = (bf16[2,384,1536]{2,1,0:T(8,128)(2,1)}, bf16[2,384,1536]{2,1,0:T(8,128)(2,1)}, u32[]{:S(2)}, u32[]{:S(2)}) collective-permute-start(bf16[2,384,1536]{2,1,0:T(8,128)(2,1)} %bitcast.67), channel_id=1, source_target_pairs={{1,0},{2,1},{3,2},{4,3},{5,4},{6,5},{7,6},{8,7},{9,8},{10,9},{11,1... | collective-permute-start | bytes 7077896 | tf_op jit(solution)/shard_map/ppermute | solution.py:29
  14.6 339.4 %copy-start.5 = (f32[1,128]{1,0:T(1,128)S(1)}, f32[1,128]{1,0:T(1,128)}, u32[]{:S(2)}) copy-start(f32[1,128]{1,0:T(1,128)} %param.23) | copy-start | bytes 1540
  355.3 17.8 %collective-permute-start = (bf16[2,128,1536]{2,1,0:T(8,128)(2,1)S(1)}, bf16[2,128,1536]{2,1,0:T(8,128)(2,1)S(1)}, u32[]{:S(2)}, u32[]{:S(2)}) collective-permute-start(bf16[2,128,1536]{2,1,0:T(8,128)(2,1)S(1)} %get-tuple-element.507), channel_id=1, source_target_pairs={{0,1},{1,2},{2,3},{3,4},{4,5},{5,6},{6,7},{7,8},{8,9},{9,10},{10,1... | collective-permute-start | bytes 2359304 | tf_op jit(solution)/shard_map/while/body/eval_jaxpr/ppermute | solution.py:27
  358.3 17.2 %collective-permute-start.1 = (bf16[2,128,1536]{2,1,0:T(8,128)(2,1)S(1)}, bf16[2,128,1536]{2,1,0:T(8,128)(2,1)S(1)}, u32[]{:S(2)}, u32[]{:S(2)}) collective-permute-start(bf16[2,128,1536]{2,1,0:T(8,128)(2,1)S(1)} %get-tuple-element.507), channel_id=1, source_target_pairs={{1,0},{2,1},{3,2},{4,3},{5,4},{6,5},{7,6},{8,7},{9,8},{10,9},{11,1... | collective-permute-start | bytes 2359304 | tf_op jit(solution)/shard_map/while/body/eval_jaxpr/ppermute | solution.py:29
  376.3 8.0 collective-permute-start.2
  385.5 15.8 %collective-permute-start = (bf16[2,128,1536]{2,1,0:T(8,128)(2,1)S(1)}, bf16[2,128,1536]{2,1,0:T(8,128)(2,1)S(1)}, u32[]{:S(2)}, u32[]{:S(2)}) collective-permute-start(bf16[2,128,1536]{2,1,0:T(8,128)(2,1)S(1)} %get-tuple-element.507), channel_id=1, source_target_pairs={{0,1},{1,2},{2,3},{3,4},{4,5},{5,6},{6,7},{7,8},{8,9},{9,10},{10,1... | collective-permute-start | bytes 2359304 | tf_op jit(solution)/shard_map/while/body/eval_jaxpr/ppermute | solution.py:27
  388.9 18.3 %collective-permute-start.1 = (bf16[2,128,1536]{2,1,0:T(8,128)(2,1)S(1)}, bf16[2,128,1536]{2,1,0:T(8,128)(2,1)S(1)}, u32[]{:S(2)}, u32[]{:S(2)}) collective-permute-start(bf16[2,128,1536]{2,1,0:T(8,128)(2,1)S(1)} %get-tuple-element.507), channel_id=1, source_target_pairs={{1,0},{2,1},{3,2},{4,3},{5,4},{6,5},{7,6},{8,7},{9,8},{10,9},{11,1... | collective-permute-start | bytes 2359304 | tf_op jit(solution)/shard_map/while/body/eval_jaxpr/ppermute | solution.py:29
  407.9 10.2 collective-permute-start.2
  419.4 13.9 %collective-permute-start = (bf16[2,128,1536]{2,1,0:T(8,128)(2,1)S(1)}, bf16[2,128,1536]{2,1,0:T(8,128)(2,1)S(1)}, u32[]{:S(2)}, u32[]{:S(2)}) collective-permute-start(bf16[2,128,1536]{2,1,0:T(8,128)(2,1)S(1)} %get-tuple-element.507), channel_id=1, source_target_pairs={{0,1},{1,2},{2,3},{3,4},{4,5},{5,6},{6,7},{7,8},{8,9},{9,10},{10,1... | collective-permute-start | bytes 2359304 | tf_op jit(solution)/shard_map/while/body/eval_jaxpr/ppermute | solution.py:27
  422.7 15.7 %collective-permute-start.1 = (bf16[2,128,1536]{2,1,0:T(8,128)(2,1)S(1)}, bf16[2,128,1536]{2,1,0:T(8,128)(2,1)S(1)}, u32[]{:S(2)}, u32[]{:S(2)}) collective-permute-start(bf16[2,128,1536]{2,1,0:T(8,128)(2,1)S(1)} %get-tuple-element.507), channel_id=1, source_target_pairs={{1,0},{2,1},{3,2},{4,3},{5,4},{6,5},{7,6},{8,7},{9,8},{10,9},{11,1... | collective-permute-start | bytes 2359304 | tf_op jit(solution)/shard_map/while/body/eval_jaxpr/ppermute | solution.py:29
  439.3 11.3 collective-permute-start.2
  451.8 14.9 %collective-permute-start = (bf16[2,128,1536]{2,1,0:T(8,128)(2,1)S(1)}, bf16[2,128,1536]{2,1,0:T(8,128)(2,1)S(1)}, u32[]{:S(2)}, u32[]{:S(2)}) collective-permute-start(bf16[2,128,1536]{2,1,0:T(8,128)(2,1)S(1)} %get-tuple-element.507), channel_id=1, source_target_pairs={{0,1},{1,2},{2,3},{3,4},{4,5},{5,6},{6,7},{7,8},{8,9},{9,10},{10,1... | collective-permute-start | bytes 2359304 | tf_op jit(solution)/shard_map/while/body/eval_jaxpr/ppermute | solution.py:27
  455.1 16.8 %collective-permute-start.1 = (bf16[2,128,1536]{2,1,0:T(8,128)(2,1)S(1)}, bf16[2,128,1536]{2,1,0:T(8,128)(2,1)S(1)}, u32[]{:S(2)}, u32[]{:S(2)}) collective-permute-start(bf16[2,128,1536]{2,1,0:T(8,128)(2,1)S(1)} %get-tuple-element.507), channel_id=1, source_target_pairs={{1,0},{2,1},{3,2},{4,3},{5,4},{6,5},{7,6},{8,7},{9,8},{10,9},{11,1... | collective-permute-start | bytes 2359304 | tf_op jit(solution)/shard_map/while/body/eval_jaxpr/ppermute | solution.py:29
  472.8 10.2 collective-permute-start.2
  484.2 14.9 %collective-permute-start = (bf16[2,128,1536]{2,1,0:T(8,128)(2,1)S(1)}, bf16[2,128,1536]{2,1,0:T(8,128)(2,1)S(1)}, u32[]{:S(2)}, u32[]{:S(2)}) collective-permute-start(bf16[2,128,1536]{2,1,0:T(8,128)(2,1)S(1)} %get-tuple-element.507), channel_id=1, source_target_pairs={{0,1},{1,2},{2,3},{3,4},{4,5},{5,6},{6,7},{7,8},{8,9},{9,10},{10,1... | collective-permute-start | bytes 2359304 | tf_op jit(solution)/shard_map/while/body/eval_jaxpr/ppermute | solution.py:27
  487.6 16.8 %collective-permute-start.1 = (bf16[2,128,1536]{2,1,0:T(8,128)(2,1)S(1)}, bf16[2,128,1536]{2,1,0:T(8,128)(2,1)S(1)}, u32[]{:S(2)}, u32[]{:S(2)}) collective-permute-start(bf16[2,128,1536]{2,1,0:T(8,128)(2,1)S(1)} %get-tuple-element.507), channel_id=1, source_target_pairs={{1,0},{2,1},{3,2},{4,3},{5,4},{6,5},{7,6},{8,7},{9,8},{10,9},{11,1... | collective-permute-start | bytes 2359304 | tf_op jit(solution)/shard_map/while/body/eval_jaxpr/ppermute | solution.py:29
  505.2 10.2 collective-permute-start.2
  516.6 14.9 %collective-permute-start = (bf16[2,128,1536]{2,1,0:T(8,128)(2,1)S(1)}, bf16[2,128,1536]{2,1,0:T(8,128)(2,1)S(1)}, u32[]{:S(2)}, u32[]{:S(2)}) collective-permute-start(bf16[2,128,1536]{2,1,0:T(8,128)(2,1)S(1)} %get-tuple-element.507), channel_id=1, source_target_pairs={{0,1},{1,2},{2,3},{3,4},{4,5},{5,6},{6,7},{7,8},{8,9},{9,10},{10,1... | collective-permute-start | bytes 2359304 | tf_op jit(solution)/shard_map/while/body/eval_jaxpr/ppermute | solution.py:27
  520.0 16.8 %collective-permute-start.1 = (bf16[2,128,1536]{2,1,0:T(8,128)(2,1)S(1)}, bf16[2,128,1536]{2,1,0:T(8,128)(2,1)S(1)}, u32[]{:S(2)}, u32[]{:S(2)}) collective-permute-start(bf16[2,128,1536]{2,1,0:T(8,128)(2,1)S(1)} %get-tuple-element.507), channel_id=1, source_target_pairs={{1,0},{2,1},{3,2},{4,3},{5,4},{6,5},{7,6},{8,7},{9,8},{10,9},{11,1... | collective-permute-start | bytes 2359304 | tf_op jit(solution)/shard_map/while/body/eval_jaxpr/ppermute | solution.py:29
  537.6 10.2 collective-permute-start.2
  549.0 12.7 collective-permute-start
  552.4 14.6 %collective-permute-start.1 = (bf16[2,128,1536]{2,1,0:T(8,128)(2,1)S(1)}, bf16[2,128,1536]{2,1,0:T(8,128)(2,1)S(1)}, u32[]{:S(2)}, u32[]{:S(2)}) collective-permute-start(bf16[2,128,1536]{2,1,0:T(8,128)(2,1)S(1)} %get-tuple-element.507), channel_id=1, source_target_pairs={{1,0},{2,1},{3,2},{4,3},{5,4},{6,5},{7,6},{8,7},{9,8},{10,9},{11,1... | collective-permute-start | bytes 2359304 | tf_op jit(solution)/shard_map/while/body/eval_jaxpr/ppermute | solution.py:29
  567.8 420.7 %collective-permute-start.2 = (bf16[128,1536]{1,0:T(8,128)(2,1)}, bf16[128,1536]{1,0:T(8,128)(2,1)S(1)}, u32[]{:S(2)}, u32[]{:S(2)}) collective-permute-start(bf16[128,1536]{1,0:T(8,128)(2,1)} %get-tuple-element.510), channel_id=1, source_target_pairs={{0,32},{32,64},{64,96},{96,128},{128,160},{160,192},{192,224},{1,3... | collective-permute-start | bytes 1179656 | tf_op jit(solution)/shard_map/while/body/eval_jaxpr/ppermute | solution.py:39
  994.2 3.8 copy-start.2
  999.5 12.7 collective-permute-start
  1003.2 14.6 %collective-permute-start.1 = (bf16[2,128,1536]{2,1,0:T(8,128)(2,1)S(1)}, bf16[2,128,1536]{2,1,0:T(8,128)(2,1)S(1)}, u32[]{:S(2)}, u32[]{:S(2)}) collective-permute-start(bf16[2,128,1536]{2,1,0:T(8,128)(2,1)S(1)} %get-tuple-element.507), channel_id=1, source_target_pairs={{1,0},{2,1},{3,2},{4,3},{5,4},{6,5},{7,6},{8,7},{9,8},{10,9},{11,1... | collective-permute-start | bytes 2359304 | tf_op jit(solution)/shard_map/while/body/eval_jaxpr/ppermute | solution.py:29
  1017.8 9.1 copy-start
  1017.8 9.1 copy-start.3
  1049.3 5.6 copy-start.4
  1059.9 7.2 slice-start
  1063.0 4.2 copy-start.1
  1063.0 4.2 slice-start.1
  1071.8 15.0 %collective-permute-start.2 = (bf16[128,1536]{1,0:T(8,128)(2,1)}, bf16[128,1536]{1,0:T(8,128)(2,1)S(1)}, u32[]{:S(2)}, u32[]{:S(2)}) collective-permute-start(bf16[128,1536]{1,0:T(8,128)(2,1)} %get-tuple-element.510), channel_id=1, source_target_pairs={{0,32},{32,64},{64,96},{96,128},{128,160},{160,192},{192,224},{1,3... | collective-permute-start | bytes 1179656 | tf_op jit(solution)/shard_map/while/body/eval_jaxpr/ppermute | solution.py:39
  1092.4 3.8 copy-start.2
  1097.8 12.7 collective-permute-start
  1101.4 14.3 %collective-permute-start.1 = (bf16[2,128,1536]{2,1,0:T(8,128)(2,1)S(1)}, bf16[2,128,1536]{2,1,0:T(8,128)(2,1)S(1)}, u32[]{:S(2)}, u32[]{:S(2)}) collective-permute-start(bf16[2,128,1536]{2,1,0:T(8,128)(2,1)S(1)} %get-tuple-element.507), channel_id=1, source_target_pairs={{1,0},{2,1},{3,2},{4,3},{5,4},{6,5},{7,6},{8,7},{9,8},{10,9},{11,1... | collective-permute-start | bytes 2359304 | tf_op jit(solution)/shard_map/while/body/eval_jaxpr/ppermute | solution.py:29
  1115.8 9.1 copy-start
  1115.8 9.1 copy-start.3
  1147.3 5.6 copy-start.4
  1158.0 7.2 slice-start
  1161.0 4.2 copy-start.1
  1161.0 4.2 slice-start.1
  1169.8 19.4 %collective-permute-start.2 = (bf16[128,1536]{1,0:T(8,128)(2,1)}, bf16[128,1536]{1,0:T(8,128)(2,1)S(1)}, u32[]{:S(2)}, u32[]{:S(2)}) collective-permute-start(bf16[128,1536]{1,0:T(8,128)(2,1)} %get-tuple-element.510), channel_id=1, source_target_pairs={{0,32},{32,64},{64,96},{96,128},{128,160},{160,192},{192,224},{1,3... | collective-permute-start | bytes 1179656 | tf_op jit(solution)/shard_map/while/body/eval_jaxpr/ppermute | solution.py:39
  1194.8 3.8 copy-start.2
  1200.2 18.1 %collective-permute-start = (bf16[2,128,1536]{2,1,0:T(8,128)(2,1)S(1)}, bf16[2,128,1536]{2,1,0:T(8,128)(2,1)S(1)}, u32[]{:S(2)}, u32[]{:S(2)}) collective-permute-start(bf16[2,128,1536]{2,1,0:T(8,128)(2,1)S(1)} %get-tuple-element.507), channel_id=1, source_target_pairs={{0,1},{1,2},{2,3},{3,4},{4,5},{5,6},{6,7},{7,8},{8,9},{9,10},{10,1... | collective-permute-start | bytes 2359304 | tf_op jit(solution)/shard_map/while/body/eval_jaxpr/ppermute | solution.py:27
  1203.8 19.4 %collective-permute-start.1 = (bf16[2,128,1536]{2,1,0:T(8,128)(2,1)S(1)}, bf16[2,128,1536]{2,1,0:T(8,128)(2,1)S(1)}, u32[]{:S(2)}, u32[]{:S(2)}) collective-permute-start(bf16[2,128,1536]{2,1,0:T(8,128)(2,1)S(1)} %get-tuple-element.507), channel_id=1, source_target_pairs={{1,0},{2,1},{3,2},{4,3},{5,4},{6,5},{7,6},{8,7},{9,8},{10,9},{11,1... | collective-permute-start | bytes 2359304 | tf_op jit(solution)/shard_map/while/body/eval_jaxpr/ppermute | solution.py:29
  1223.2 9.1 copy-start
  1223.2 9.1 copy-start.3
  1254.6 5.6 copy-start.4
  1265.3 7.2 slice-start
  1268.3 4.2 copy-start.1
  1268.3 4.2 slice-start.1
  1277.0 3.8 collective-permute-start.2
Sparse Core Ops, SparseCore 0:
  9.9 88.7 all-gather.8
  101.3 84.8 all-gather.10
  188.8 80.7 all-gather.12
  272.1 80.7 all-gather.14
where the time goes:
time: 1290 us
  waiting for transfers between devices  986 us (76%)
  local copies, waits for them, and re-layouts  128 us (10%)
  starting transfers between devices  72.7 us (6%)
  matrix products  52.2 us (4%)
  other arithmetic  34.5 us (3%)
  between operations  13.2 us (1%)
    ppermute x10, waiting for transfers between devices, from_behind(): return lax.ppermute(value, axis, pairs)  506 us
    ppermute x11, waiting for transfers between devices, extended(): lax.ppermute(tail, axis, [(i, (i + 1) % count) for i in range(ends)])  148 us
    all_gather x1, waiting for transfers between devices, per_device(): lax.all_gather(key_weight[0], 'seq', axis=0, tiled=True)  87.5 us
    all_gather x1, waiting for transfers between devices, per_device(): lax.all_gather(value_weight[0], 'seq', axis=0, tiled=True)  83.4 us
    all_gather x1, waiting for transfers between devices, per_device(): lax.all_gather(out_weight[0], 'seq', axis=0, tiled=True)  83.3 us
    ppermute x11, waiting for transfers between devices, extended(): lax.ppermute(head, axis, [((i + 1) % count, i) for i in range(ends)])  55.1 us
    ppermute x11, starting transfers between devices, extended(): lax.ppermute(tail, axis, [(i, (i + 1) % count) for i in range(ends)])  37.3 us
  transfers between devices with their start and end apart: 36, of which 36 were waited for; matrix products, arithmetic and copies ran while one was open for 0% of the time, Pallas kernels for 0%

commit v1 on v0

v1 whole, which is shorter than its diff:
```python
import functools
import math

import jax
import jax.numpy as jnp
from jax import lax
from jax.experimental import pallas as pl
from jax.experimental.pallas import tpu as pltpu
from jax.sharding import PartitionSpec as P

D = 1536
HEADS = 12
HEAD = 128
TILE = 64
KT = 6
PATCHES = 3
TPP = 2
TPD = 6
ROWS = TPP * TILE
PAIR = 2 * HEAD
BLOCKS = 8
SKEW = 1
EPSILON = 1e-06
SCALE = math.log2(math.e) / math.sqrt(HEAD)
AXES = ("segment", "seq")
VMEM = pl.BlockSpec(memory_space=pltpu.VMEM)
SMEM = pl.BlockSpec(memory_space=pltpu.SMEM)


def head_normed(projected, gain):
    parts = []
    for h in range(projected.shape[1] // HEAD):
        head = projected[:, h * HEAD : (h + 1) * HEAD]
        mean = jnp.mean(head * head, axis=-1, keepdims=True)
        parts.append((head * lax.rsqrt(mean + EPSILON) * gain).astype(jnp.bfloat16))
    return jnp.concatenate(parts, axis=1)


def round_kernel(
    slot,
    with_latent,
    mask_ref,
    gain_q_ref,
    gain_k_ref,
    weights_ref,
    own_ref,
    behind_ref,
    ahead_ref,
    keys_in,
    values_in,
    result_in,
    *rest,
):
    if with_latent:
        latent_ref, *rest = rest
    leaving_ref, keys_ref, values_ref, result_ref, inputs, attended, listed = rest
    block = lax.axis_index("segment")
    frame = lax.axis_index("seq")
    patch = slot - SKEW * block

    @pl.when((patch >= 0) & (patch < PATCHES))
    def _():
        for f, received in enumerate((behind_ref, own_ref, ahead_ref)):
            rows = pl.ds(f * ROWS, ROWS)
            if with_latent:

                @pl.when(block == 0)
                def _(f=f, rows=rows):
                    inputs[rows, :] = latent_ref[f]

                @pl.when(block != 0)
                def _(received=received, rows=rows):
                    inputs[rows, :] = received[...]
            else:
                inputs[rows, :] = received[...]
        lists = []
        slot_of = lax.broadcasted_iota(jnp.int32, (TILE, KT * TILE), 1) // TILE
        for i in range(TPP):
            entries = []
            usable = jnp.zeros((TILE, KT * TILE), jnp.float32)
            for m in range(KT):
                tile = mask_ref[patch * TPP + i, m]
                entries.append(jnp.where(tile >= 0, tile - (frame - 1) * TPD, 0))
                here = jnp.where(tile >= 0, 1.0, 0.0)
                usable = jnp.where(slot_of == m, here, usable)
            lists.append(entries)
            listed[i] = usable

        def weight(j, columns):
            return weights_ref[:, j, :, columns].reshape(D, PAIR)

        def dot(a, b):
            return jnp.dot(a, b, preferred_element_type=jnp.float32)

        def head_pair(c, carry):
            columns = pl.ds(pl.multiple_of(c * PAIR, PAIR), PAIR)
            fresh_k = head_normed(dot(inputs[...], weight(1, columns)), gain_k_ref[...])
            fresh_v = dot(inputs[...], weight(2, columns)).astype(jnp.bfloat16)
            fresh_q = head_normed(dot(inputs[pl.ds(ROWS, ROWS), :], weight(0, columns)), gain_q_ref[...])
            for f in range(3):
                rows = slice(f * ROWS, (f + 1) * ROWS)
                tiles = pl.ds(f * TPD + patch * TPP, TPP)
                keys_ref[tiles, :, columns] = fresh_k[rows].reshape(TPP, TILE, PAIR)
                values_ref[tiles, :, columns] = fresh_v[rows].reshape(TPP, TILE, PAIR)
            for i in range(TPP):
                k = jnp.concatenate([keys_ref[t, :, columns] for t in lists[i]], axis=0)
                v = jnp.concatenate([values_ref[t, :, columns] for t in lists[i]], axis=0)
                outs = []
                for h in range(2):
                    head = slice(h * HEAD, (h + 1) * HEAD)
                    q = fresh_q[i * TILE : (i + 1) * TILE, head]
                    scores = lax.dot_general(
                        q, k[:, head], (((1,), (1,)), ((), ())), preferred_element_type=jnp.float32
                    )
                    weights = jnp.where(listed[i] > 0.0, jnp.exp2(scores * SCALE), 0.0)
                    total = jnp.sum(weights, axis=-1, keepdims=True)
                    outs.append(dot(weights.astype(jnp.bfloat16), v[:, head]) / total)
                attended[pl.ds(i * TILE, TILE), columns] = jnp.concatenate(outs, axis=1).astype(jnp.bfloat16)
            return carry

        lax.fori_loop(0, D // PAIR, head_pair, 0, unroll=True)

        def mix(c, carry):
            columns = pl.ds(pl.multiple_of(c * PAIR, PAIR), PAIR)
            mixed = dot(attended[...], weight(3, columns))
            leaving = (inputs[pl.ds(ROWS, ROWS), columns].astype(jnp.float32) + mixed).astype(jnp.bfloat16)
            leaving_ref[:, columns] = leaving
            result_ref[patch, :, columns] = leaving
            return carry

        lax.fori_loop(0, D // PAIR, mix, 0, unroll=True)


def run_round(slot, mask, gain_q, gain_k, weights, own, behind, ahead, keys, values, result, latent):
    with_latent = latent is not None
    operands = [mask, gain_q, gain_k, weights, own, behind, ahead, keys, values, result]
    if with_latent:
        operands.append(latent)
    operands = operands[:1] + [pltpu.with_memory_space_constraint(o, pltpu.VMEM) for o in operands[1:]]
    return pl.pallas_call(
        functools.partial(round_kernel, slot, with_latent),
        out_shape=(
            jax.ShapeDtypeStruct((ROWS, D), jnp.bfloat16),
            jax.ShapeDtypeStruct(keys.shape, keys.dtype),
            jax.ShapeDtypeStruct(values.shape, values.dtype),
            jax.ShapeDtypeStruct(result.shape, result.dtype),
        ),
        in_specs=[SMEM] + [VMEM] * (len(operands) - 1),
        out_specs=(VMEM,) * 4,
        input_output_aliases={7: 1, 8: 2, 9: 3},
        scratch_shapes=[
            pltpu.VMEM((3 * ROWS, D), jnp.bfloat16),
            pltpu.VMEM((ROWS, D), jnp.bfloat16),
            pltpu.VMEM((TPP, TILE, KT * TILE), jnp.float32),
        ],
        compiler_params=pltpu.CompilerParams(vmem_limit_bytes=16 << 20),
        name="round",
    )(*operands)


def device_of(block, frame, frames):
    return block * frames + frame


def per_device(
    latent,
    stale_kv,
    query_weight,
    key_weight,
    value_weight,
    out_weight,
    query_gain,
    key_gain,
    tile_mask,
):
    frames = lax.axis_size("seq")

    def send(value, blocks, hop, by):
        pairs = [
            (device_of(b, t, frames), device_of(b + hop, t + by, frames))
            for b in blocks
            for t in range(frames)
            if 0 <= t + by < frames
        ]
        return lax.ppermute(value, AXES, pairs)

    everyone = range(BLOCKS)
    shard = jnp.concatenate([query_weight, key_weight, value_weight, out_weight], axis=0)
    weights = lax.all_gather(shard, "seq", axis=0)

    latent3 = jnp.stack([send(latent, [0], 0, 1), latent, send(latent, [0], 0, -1)])
    latent3 = latent3.reshape(3, PATCHES, ROWS, D)
    local = stale_kv[0]
    late = local[:, ROWS:]
    unread = jnp.zeros((2, ROWS, D), jnp.bfloat16)
    window = jnp.stack(
        [
            jnp.concatenate([unread, send(late, everyone, 0, 1)], axis=1),
            local,
            jnp.concatenate([unread, send(late, everyone, 0, -1)], axis=1),
        ],
        axis=1,
    ).reshape(2, 3 * TPD, TILE, D)
    keys, values = window[0], window[1]
    result = jnp.zeros((PATCHES, ROWS, D), jnp.bfloat16)
    empty = jnp.zeros((ROWS, D), jnp.bfloat16)

    last = SKEW * (BLOCKS - 1) + PATCHES - 1
    arrived = {s: (empty, empty, empty) for s in range(SKEW)}
    for slot in range(last + 1):
        own, behind, ahead = arrived[slot]
        leaving, keys, values, result = run_round(
            slot,
            tile_mask,
            query_gain,
            key_gain,
            weights,
            own,
            behind,
            ahead,
            keys,
            values,
            result,
            latent3[:, slot] if slot < PATCHES else None,
        )
        blocks = [b for b in range(BLOCKS - 1) if 0 <= slot - SKEW * b < PATCHES]
        if blocks:
            arrived[slot + SKEW] = tuple(send(leaving, blocks, 1, by) for by in (0, 1, -1))
    return result.reshape(1, PATCHES * ROWS, D)


def solution(mesh):
    return jax.shard_map(
        per_device,
        mesh=mesh,
        in_specs=(
            P("seq", None),
            P("segment", None, "seq", None),
            P("segment", "seq", None),
            P("segment", "seq", None),
            P("segment", "seq", None),
            P("segment", "seq", None),
            P("segment", None),
            P("segment", None),
            P("seq", None),
        ),
        out_specs=P("segment", "seq", None),
        check_vma=False,
    )
```

time: 1290 us -> 446 us (0.35)
  waiting for transfers between devices: 986 us -> 323 us
  local copies, waits for them, and re-layouts: 128 us -> 17.1 us
  matrix products: 52.2 us -> 0 us
  Pallas kernels: 0 us -> 50.1 us
  starting transfers between devices: 72.7 us -> 30.7 us
  other arithmetic: 34.5 us -> 3.44 us
    ppermute x32 -> x31, waiting for transfers between devices: 709 us -> 210 us  [send(): return lax.ppermute(value, AXES, pairs)]
    all_gather x4 -> x1, waiting for transfers between devices: 273 us -> 113 us  [per_device(): weights = lax.all_gather(shard, 'seq', axis=0)]
    dot_general x18 -> x0, matrix products: 52.2 us -> none  [the longest x3 14.2 us: attend(): jnp.einsum('pthe,pkhe->phtk', query_heads, key_heads, preferred_element_t...]
    pallas_call x0 -> x10, Pallas kernels: none -> 50.1 us  [run_round(): pl.pallas_call(functools.partial(round_kernel, slot, with_latent), out_sh...]
    dynamic_update_slice x12 -> x0, local copies, waits for them, and re-layouts: 49.6 us -> none  [the longest x3 13.9 us: finish(): updated = lax.dynamic_update_slice_in_dim(former, trailing, offset, 1)]
    ppermute x32 -> x31, starting transfers between devices: 72.6 us -> 30.7 us  [send(): return lax.ppermute(value, AXES, pairs)]
    reshape x9 -> x0, local copies, waits for them, and re-layouts: 26.4 us -> none  [the longest x3 16.4 us: attend(): jnp.take(blocks[0], tile_index, axis=0).reshape(n_query, -1, HEADS, HEAD)]
    select_n x13 -> x0, other arithmetic: 23.6 us -> none  [the longest x3 12.7 us: attend(): jnp.take(blocks[0], tile_index, axis=0).reshape(n_query, -1, HEADS, HEAD)]
  transfers between devices with their start and end apart: 36 -> 32, of which waited for: 36 -> 9; matrix products, arithmetic and copies ran while one was open for 0% -> 2% of each run, Pallas kernels for 0% -> 0%
where the time goes in v1:
time: 446 us; the launch traced here: 438 us
  waiting for transfers between devices  323 us (72%)
  Pallas kernels  50.1 us (11%)
  starting transfers between devices  30.7 us (7%)
  local copies, waits for them, and re-layouts  17.1 us (4%)
  between operations  14.3 us (3%)
    ppermute x31, waiting for transfers between devices, send(): return lax.ppermute(value, AXES, pairs)  210 us
    all_gather x1, waiting for transfers between devices, per_device(): weights = lax.all_gather(shard, 'seq', axis=0)  113 us
    pallas_call x10, Pallas kernels, run_round(): pl.pallas_call(functools.partial(round_kernel, slot, with_latent), out_sh...  50.1 us
    ppermute x31, starting transfers between devices, send(): return lax.ppermute(value, AXES, pairs)  30.7 us
    unnamed x21, local copies, waits for them, and re-layouts  10.7 us
  transfers between devices with their start and end apart: 32, of which 9 were waited for; matrix products, arithmetic and copies ran while one was open for 2% of the time, Pallas kernels for 0%

profile of v1, /device:TPU:111, one launch (start us, length us, event | category | flops | bytes accessed | tf_op | source)
XLA Modules:
  0.0 438.3 jit_solution(15223852491210655622)
XLA Ops:
  6.5 2.2 pad_maximum_fusion.2
  8.7 0.0 all-gather.3.cloned.1.call-update
  8.7 0.7 collective-permute-start.2
  9.5 0.7 collective-permute-start.3
  10.2 1.5 slice.26
  11.8 2.1 collective-permute-start.1
  13.8 3.2 collective-permute-start
  17.1 0.4 pad_maximum_fusion.1
  17.5 2.0 slice_bitcast_fusion
  19.5 38.9 %collective-permute-done.1 = bf16[2,256,1536]{2,1,0:T(8,128)(2,1)S(1)} collective-permute-done((bf16[2,256,1536]{2,1,0:T(8,128)(2,1)S(1)}, bf16[2,256,1536]{2,1,0:T(8,128)(2,1)S(1)}, u32[]{:S(2)}, u32[]{:S(2)}) %collective-permute-start.1) | collective-permute-done | bytes 1572896 | tf_op jit(solution)/shard_map/ppermute | solution.py:185
  58.4 0.2 pad_bitcast_fusion
  58.5 2.8 collective-permute-done
  61.3 0.2 pad_bitcast_fusion.1
  61.5 0.8 pad_maximum_fusion
  62.3 2.6 fusion
  64.9 112.9 %all-gather.3.cloned.1.call-done = bf16[128,48,1536]{2,1,0:T(8,128)(2,1)} async-done(((bf16[4,48,1536]{2,1,0:T(8,128)(2,1)}), bf16[128,48,1536]{2,1,0:T(8,128)(2,1)}) %all-gather.3.cloned.1.call-update) | async-done | bytes 18874384 | tf_op jit(solution)/shard_map/all_gather | solution.py:189
  177.9 0.1 broadcast_in_dim.8.result_in
  178.0 6.4 %copy-done = bf16[128,48,1536]{2,1,0:T(8,128)(2,1)S(1)} copy-done((bf16[128,48,1536]{2,1,0:T(8,128)(2,1)S(1)}, bf16[128,48,1536]{2,1,0:T(8,128)(2,1)}, u32[]{:S(2)}) %copy-start) | copy-done | bytes 18874392
  184.4 2.0 copy-done.1
  186.4 1.3 copy-done.4
  187.6 0.6 round.10
  188.3 0.7 collective-permute-start.6
  189.0 0.7 collective-permute-start.5
  189.7 0.7 collective-permute-start.4
  190.4 6.7 %round.11 = (bf16[128,1536]{1,0:T(8,128)(2,1)S(1)}, bf16[18,64,1536]{2,1,0:T(8,128)(2,1)S(1)}, bf16[18,64,1536]{2,1,0:T(8,128)(2,1)S(1)}, bf16[3,128,1536]{2,1,0:T(8,128)(2,1)S(1)}) custom-call(s32[6,6]{1,0:T(8,128)S(1)} %copy-done.5, f32[1,128]{1,0:T(1,128)S(1)} %copy-done.6, ...), custom_call_target="tpu_custom_call", output_to_operand_aliasing={{1}: (7, {}), {2}: (8, {}), {3}: (9, {})} | custom-call | tf_op jit(solution)/shard_map/round/pallas_call | solution.py:140
  197.1 0.7 collective-permute-start.9
  197.8 0.7 collective-permute-start.8
  198.5 0.7 collective-permute-start.7
  199.2 0.6 round.12
  199.9 0.7 collective-permute-start.12
  200.6 0.7 collective-permute-start.11
  201.3 0.7 collective-permute-start.10
  202.0 0.8 round.13
  202.8 0.7 collective-permute-start.15
  203.5 0.7 collective-permute-start.14
  204.2 0.7 collective-permute-start.13
  204.9 3.4 round.14
  208.3 0.7 collective-permute-start.18
  209.0 0.7 collective-permute-start.17
  209.7 0.7 collective-permute-start.16
  210.4 3.4 round.15
  213.8 0.7 collective-permute-start.21
  214.5 0.7 collective-permute-start.20
  215.2 0.7 collective-permute-start.19
  216.0 3.6 round.16
  219.6 1.3 collective-permute-start.24
  220.9 1.3 collective-permute-start.23
  222.2 1.3 collective-permute-start.22
  223.5 138.9 %collective-permute-done.24.ahead_ref = bf16[128,1536]{1,0:T(8,128)(2,1)S(1)} collective-permute-done((bf16[128,1536]{1,0:T(8,128)(2,1)S(1)}, bf16[128,1536]{1,0:T(8,128)(2,1)S(1)}, u32[]{:S(2)}, u32[]{:S(2)}) %collective-permute-start.24) | collective-permute-done | bytes 393248 | tf_op jit(solution)/shard_map/ppermute | solution.py:185
  362.4 3.3 collective-permute-done.23.behind_ref
  365.6 10.0 %round.17 = (bf16[128,1536]{1,0:T(8,128)(2,1)S(1)}, bf16[18,64,1536]{2,1,0:T(8,128)(2,1)S(1)}, bf16[18,64,1536]{2,1,0:T(8,128)(2,1)S(1)}, bf16[3,128,1536]{2,1,0:T(8,128)(2,1)S(1)}) custom-call(s32[6,6]{1,0:T(8,128)S(1)} %copy-done.5, f32[1,128]{1,0:T(1,128)S(1)} %copy-done.6, ...), custom_call_target="tpu_custom_call", output_to_operand_aliasing={{1}: (7, {}), {2}: (8, {}), {3}: (9, {})} | custom-call | tf_op jit(solution)/shard_map/round/pallas_call | solution.py:140
  375.7 1.3 collective-permute-start.27
  377.0 1.3 collective-permute-start.26
  378.3 1.3 collective-permute-start.25
  379.6 5.3 %collective-permute-done.27.ahead_ref = bf16[128,1536]{1,0:T(8,128)(2,1)S(1)} collective-permute-done((bf16[128,1536]{1,0:T(8,128)(2,1)S(1)}, bf16[128,1536]{1,0:T(8,128)(2,1)S(1)}, u32[]{:S(2)}, u32[]{:S(2)}) %collective-permute-start.27) | collective-permute-done | bytes 393248 | tf_op jit(solution)/shard_map/ppermute | solution.py:185
  384.9 6.0 %collective-permute-done.26.behind_ref = bf16[128,1536]{1,0:T(8,128)(2,1)S(1)} collective-permute-done((bf16[128,1536]{1,0:T(8,128)(2,1)S(1)}, bf16[128,1536]{1,0:T(8,128)(2,1)S(1)}, u32[]{:S(2)}, u32[]{:S(2)}) %collective-permute-start.26) | collective-permute-done | bytes 393248 | tf_op jit(solution)/shard_map/ppermute | solution.py:185
  391.0 10.1 %round.18 = (bf16[128,1536]{1,0:T(8,128)(2,1)S(1)}, bf16[18,64,1536]{2,1,0:T(8,128)(2,1)S(1)}, bf16[18,64,1536]{2,1,0:T(8,128)(2,1)S(1)}, bf16[3,128,1536]{2,1,0:T(8,128)(2,1)S(1)}) custom-call(s32[6,6]{1,0:T(8,128)S(1)} %copy-done.5, f32[1,128]{1,0:T(1,128)S(1)} %copy-done.6, ...), custom_call_target="tpu_custom_call", output_to_operand_aliasing={{1}: (7, {}), {2}: (8, {}), {3}: (9, {})} | custom-call | tf_op jit(solution)/shard_map/round/pallas_call | solution.py:140
  401.0 1.3 collective-permute-start.30
  402.3 1.3 collective-permute-start.29
  403.6 1.3 collective-permute-start.28
  404.9 11.1 %collective-permute-done.30.ahead_ref = bf16[128,1536]{1,0:T(8,128)(2,1)S(1)} collective-permute-done((bf16[128,1536]{1,0:T(8,128)(2,1)S(1)}, bf16[128,1536]{1,0:T(8,128)(2,1)S(1)}, u32[]{:S(2)}, u32[]{:S(2)}) %collective-permute-start.30) | collective-permute-done | bytes 393248 | tf_op jit(solution)/shard_map/ppermute | solution.py:185
  416.1 3.3 collective-permute-done.29.behind_ref
  419.3 10.9 %round.19 = (bf16[128,1536]{1,0:T(8,128)(2,1)}, bf16[18,64,1536]{2,1,0:T(8,128)(2,1)S(1)}, bf16[18,64,1536]{2,1,0:T(8,128)(2,1)S(1)}, bf16[3,128,1536]{2,1,0:T(8,128)(2,1)S(1)}) custom-call(s32[6,6]{1,0:T(8,128)S(1)} %copy-done.5, f32[1,128]{1,0:T(1,128)S(1)} %copy-done.6, ...), custom_call_target="tpu_custom_call", output_to_operand_aliasing={{1}: (7, {}), {2}: (8, {}), {3}: (9, {})} | custom-call | tf_op jit(solution)/shard_map/round/pallas_call | solution.py:140
  430.2 1.0 copy.70
  (42 shorter events, 0.1 us)
Async XLA Ops:
  6.5 10.5 %copy-start.9 = (bf16[384,1536]{1,0:T(8,128)(2,1)S(1)}, bf16[384,1536]{1,0:T(8,128)(2,1)}, u32[]{:S(2)}) copy-start(bf16[384,1536]{1,0:T(8,128)(2,1)} %param.9) | copy-start | bytes 3538948
  6.5 171.3 %all-gather.3.cloned.1.call-start = ((), (), s32[]{:S(2)}) async-start(), calls=%async_computation | async-start | bytes 19464192 | tf_op jit(solution)/shard_map/all_gather | solution.py:189
  8.7 8.3 %collective-permute-start.2 = (bf16[384,1536]{1,0:T(8,128)(2,1)}, bf16[384,1536]{1,0:T(8,128)(2,1)S(1)}, u32[]{:S(2)}, u32[]{:S(2)}) collective-permute-start(bf16[384,1536]{1,0:T(8,128)(2,1)} %param.9), channel_id=1, source_target_pairs={{0,1},{1,2},{2,3},{3,4},{4,5},{5,6},{6,7},{7,8},{8,9},{9,10},{10,1... | collective-permute-start | bytes 3538952 | tf_op jit(solution)/shard_map/ppermute | solution.py:185
  9.5 7.6 %collective-permute-start.3 = (bf16[384,1536]{1,0:T(8,128)(2,1)}, bf16[384,1536]{1,0:T(8,128)(2,1)S(1)}, u32[]{:S(2)}, u32[]{:S(2)}) collective-permute-start(bf16[384,1536]{1,0:T(8,128)(2,1)} %param.9), channel_id=1, source_target_pairs={{1,0},{2,1},{3,2},{4,3},{5,4},{6,5},{7,6},{8,7},{9,8},{10,9},{11,1... | collective-permute-start | bytes 3538952 | tf_op jit(solution)/shard_map/ppermute | solution.py:185
  11.8 46.6 %collective-permute-start.1 = (bf16[2,256,1536]{2,1,0:T(8,128)(2,1)S(1)}, bf16[2,256,1536]{2,1,0:T(8,128)(2,1)S(1)}, u32[]{:S(2)}, u32[]{:S(2)}) collective-permute-start(bf16[2,256,1536]{2,1,0:T(8,128)(2,1)S(1)} %slice.26), channel_id=1, source_target_pairs={{1,0},{2,1},{3,2},{4,3},{5,4},{6,5},{7,6},{8,7},{9,8},{10,9},{11,1... | collective-permute-start | bytes 4718600 | tf_op jit(solution)/shard_map/ppermute | solution.py:185
  13.8 47.5 %collective-permute-start = (bf16[2,256,1536]{2,1,0:T(8,128)(2,1)S(1)}, bf16[2,256,1536]{2,1,0:T(8,128)(2,1)S(1)}, u32[]{:S(2)}, u32[]{:S(2)}) collective-permute-start(bf16[2,256,1536]{2,1,0:T(8,128)(2,1)S(1)} %slice.26), channel_id=1, source_target_pairs={{0,1},{1,2},{2,3},{3,4},{4,5},{5,6},{6,7},{7,8},{8,9},{9,10},{10,1... | collective-permute-start | bytes 4718600 | tf_op jit(solution)/shard_map/ppermute | solution.py:185
  19.5 42.0 %copy-start.8 = (bf16[1,2,384,1536]{3,2,1,0:T(8,128)(2,1)S(1)}, bf16[1,2,384,1536]{3,2,1,0:T(8,128)(2,1)}, u32[]{:S(2)}) copy-start(bf16[1,2,384,1536]{3,2,1,0:T(8,128)(2,1)} %param.10) | copy-start | bytes 7077892
  62.3 115.7 %copy-start.5 = (s32[6,6]{1,0:T(8,128)S(1)}, s32[6,6]{1,0:T(8,128)}, u32[]{:S(2)}) copy-start(s32[6,6]{1,0:T(8,128)} %mask_ref.19) | copy-start | bytes 436
  62.3 115.7 %copy-start.6 = (f32[1,128]{1,0:T(1,128)S(1)}, f32[1,128]{1,0:T(1,128)}, u32[]{:S(2)}) copy-start(f32[1,128]{1,0:T(1,128)} %gain_q_ref.19) | copy-start | bytes 1540
  62.3 115.7 %copy-start.7 = (f32[1,128]{1,0:T(1,128)S(1)}, f32[1,128]{1,0:T(1,128)}, u32[]{:S(2)}) copy-start(f32[1,128]{1,0:T(1,128)} %gain_k_ref.19) | copy-start | bytes 1540
  178.0 6.4 %copy-start = (bf16[128,48,1536]{2,1,0:T(8,128)(2,1)S(1)}, bf16[128,48,1536]{2,1,0:T(8,128)(2,1)}, u32[]{:S(2)}) copy-start(bf16[128,48,1536]{2,1,0:T(8,128)(2,1)} %all-gather.3.cloned.1.call-done) | copy-start | bytes 56623108
  184.4 2.0 copy-start.1
  186.4 1.3 copy-start.4
  187.6 2.7 copy-start.3
  188.3 2.1 collective-permute-start.6
  189.0 1.4 collective-permute-start.5
  189.7 0.7 collective-permute-start.4
  190.4 8.9 %copy-start.2 = (bf16[3,128,1536]{2,1,0:T(8,128)(2,1)S(1)}, bf16[3,128,1536]{2,1,0:T(8,128)(2,1)}, u32[]{:S(2)}) copy-start(bf16[3,128,1536]{2,1,0:T(8,128)(2,1)} %get-tuple-element.81.rest_0_) | copy-start | bytes 3538948
  197.1 2.1 collective-permute-start.9
  197.8 1.4 collective-permute-start.8
  198.5 0.7 collective-permute-start.7
  199.9 2.1 collective-permute-start.12
  200.6 1.4 collective-permute-start.11
  201.3 0.7 collective-permute-start.10
  202.8 2.1 collective-permute-start.15
  203.5 1.4 collective-permute-start.14
  204.2 0.7 collective-permute-start.13
  208.3 2.1 collective-permute-start.18
  209.0 1.4 collective-permute-start.17
  209.7 0.7 collective-permute-start.16
  213.8 2.1 collective-permute-start.21
  214.5 1.4 collective-permute-start.20
  215.2 0.7 collective-permute-start.19
  219.6 142.8 %collective-permute-start.24 = (bf16[128,1536]{1,0:T(8,128)(2,1)S(1)}, bf16[128,1536]{1,0:T(8,128)(2,1)S(1)}, u32[]{:S(2)}, u32[]{:S(2)}) collective-permute-start(bf16[128,1536]{1,0:T(8,128)(2,1)S(1)} %get-tuple-element.66), channel_id=1, source_target_pairs={{129,160},{130,161},{131,162},{132,163},{133,164},{134,165},{135,1... | collective-permute-start | bytes 1179656 | tf_op jit(solution)/shard_map/ppermute | solution.py:185
  220.9 144.7 %collective-permute-start.23 = (bf16[128,1536]{1,0:T(8,128)(2,1)S(1)}, bf16[128,1536]{1,0:T(8,128)(2,1)S(1)}, u32[]{:S(2)}, u32[]{:S(2)}) collective-permute-start(bf16[128,1536]{1,0:T(8,128)(2,1)S(1)} %get-tuple-element.66), channel_id=1, source_target_pairs={{128,161},{129,162},{130,163},{131,164},{132,165},{133,166},{134,1... | collective-permute-start | bytes 1179656 | tf_op jit(solution)/shard_map/ppermute | solution.py:185
  222.2 143.4 %collective-permute-start.22 = (bf16[128,1536]{1,0:T(8,128)(2,1)S(1)}, bf16[128,1536]{1,0:T(8,128)(2,1)S(1)}, u32[]{:S(2)}, u32[]{:S(2)}) collective-permute-start(bf16[128,1536]{1,0:T(8,128)(2,1)S(1)} %get-tuple-element.66), channel_id=1, source_target_pairs={{128,160},{129,161},{130,162},{131,163},{132,164},{133,165},{134,1... | collective-permute-start | bytes 1179656 | tf_op jit(solution)/shard_map/ppermute | solution.py:185
  375.7 9.2 %collective-permute-start.27 = (bf16[128,1536]{1,0:T(8,128)(2,1)S(1)}, bf16[128,1536]{1,0:T(8,128)(2,1)S(1)}, u32[]{:S(2)}, u32[]{:S(2)}) collective-permute-start(bf16[128,1536]{1,0:T(8,128)(2,1)S(1)} %get-tuple-element.70), channel_id=1, source_target_pairs={{161,192},{162,193},{163,194},{164,195},{165,196},{166,197},{167,1... | collective-permute-start | bytes 1179656 | tf_op jit(solution)/shard_map/ppermute | solution.py:185
  377.0 14.0 %collective-permute-start.26 = (bf16[128,1536]{1,0:T(8,128)(2,1)S(1)}, bf16[128,1536]{1,0:T(8,128)(2,1)S(1)}, u32[]{:S(2)}, u32[]{:S(2)}) collective-permute-start(bf16[128,1536]{1,0:T(8,128)(2,1)S(1)} %get-tuple-element.70), channel_id=1, source_target_pairs={{160,193},{161,194},{162,195},{163,196},{164,197},{165,198},{166,1... | collective-permute-start | bytes 1179656 | tf_op jit(solution)/shard_map/ppermute | solution.py:185
  378.3 12.7 %collective-permute-start.25 = (bf16[128,1536]{1,0:T(8,128)(2,1)S(1)}, bf16[128,1536]{1,0:T(8,128)(2,1)S(1)}, u32[]{:S(2)}, u32[]{:S(2)}) collective-permute-start(bf16[128,1536]{1,0:T(8,128)(2,1)S(1)} %get-tuple-element.70), channel_id=1, source_target_pairs={{160,192},{161,193},{162,194},{163,195},{164,196},{165,197},{166,1... | collective-permute-start | bytes 1179656 | tf_op jit(solution)/shard_map/ppermute | solution.py:185
  401.0 15.0 %collective-permute-start.30 = (bf16[128,1536]{1,0:T(8,128)(2,1)S(1)}, bf16[128,1536]{1,0:T(8,128)(2,1)S(1)}, u32[]{:S(2)}, u32[]{:S(2)}) collective-permute-start(bf16[128,1536]{1,0:T(8,128)(2,1)S(1)} %get-tuple-element.74), channel_id=1, source_target_pairs={{193,224},{194,225},{195,226},{196,227},{197,228},{198,229},{199,2... | collective-permute-start | bytes 1179656 | tf_op jit(solution)/shard_map/ppermute | solution.py:185
  402.3 17.0 %collective-permute-start.29 = (bf16[128,1536]{1,0:T(8,128)(2,1)S(1)}, bf16[128,1536]{1,0:T(8,128)(2,1)S(1)}, u32[]{:S(2)}, u32[]{:S(2)}) collective-permute-start(bf16[128,1536]{1,0:T(8,128)(2,1)S(1)} %get-tuple-element.74), channel_id=1, source_target_pairs={{192,225},{193,226},{194,227},{195,228},{196,229},{197,230},{198,2... | collective-permute-start | bytes 1179656 | tf_op jit(solution)/shard_map/ppermute | solution.py:185
  403.6 15.7 %collective-permute-start.28 = (bf16[128,1536]{1,0:T(8,128)(2,1)S(1)}, bf16[128,1536]{1,0:T(8,128)(2,1)S(1)}, u32[]{:S(2)}, u32[]{:S(2)}) collective-permute-start(bf16[128,1536]{1,0:T(8,128)(2,1)S(1)} %get-tuple-element.74), channel_id=1, source_target_pairs={{192,224},{193,225},{194,226},{195,227},{196,228},{197,229},{198,2... | collective-permute-start | bytes 1179656 | tf_op jit(solution)/shard_map/ppermute | solution.py:185
Sparse Core Ops, SparseCore 0:
  9.9 167.8 all-gather.2

commit v2 on v1

--- a/solution.py
+++ b/solution.py
@@ -102,13 +102,21 @@
                 tiles = pl.ds(f * TPD + patch * TPP, TPP)
                 keys_ref[tiles, :, columns] = fresh_k[rows].reshape(TPP, TILE, PAIR)
                 values_ref[tiles, :, columns] = fresh_v[rows].reshape(TPP, TILE, PAIR)
+            attended[:, columns] = fresh_q
+            return carry
+
+        lax.fori_loop(0, D // PAIR, head_pair, 0, unroll=True)
+
+        def attend_pair(c, carry):
+            columns = pl.ds(pl.multiple_of(c * PAIR, PAIR), PAIR)
             for i in range(TPP):
                 k = jnp.concatenate([keys_ref[t, :, columns] for t in lists[i]], axis=0)
                 v = jnp.concatenate([values_ref[t, :, columns] for t in lists[i]], axis=0)
+                queries = attended[pl.ds(i * TILE, TILE), columns]
                 outs = []
                 for h in range(2):
                     head = slice(h * HEAD, (h + 1) * HEAD)
-                    q = fresh_q[i * TILE : (i + 1) * TILE, head]
+                    q = queries[:, head]
                     scores = lax.dot_general(
                         q, k[:, head], (((1,), (1,)), ((), ())), preferred_element_type=jnp.float32
                     )
@@ -118,7 +126,7 @@
                 attended[pl.ds(i * TILE, TILE), columns] = jnp.concatenate(outs, axis=1).astype(jnp.bfloat16)
             return carry
 
-        lax.fori_loop(0, D // PAIR, head_pair, 0, unroll=True)
+        lax.fori_loop(0, D // PAIR, attend_pair, 0, unroll=True)
 
         def mix(c, carry):
             columns = pl.ds(pl.multiple_of(c * PAIR, PAIR), PAIR)

time: 446 us -> 448 us (level)
  no operation moved by 1% of the time
where the time goes in v2:
time: 448 us; the launch traced here: 440 us
  waiting for transfers between devices  326 us (73%)
  Pallas kernels  48.3 us (11%)
  starting transfers between devices  30.7 us (7%)
  local copies, waits for them, and re-layouts  17.1 us (4%)
  between operations  14.6 us (3%)
    ppermute x31, waiting for transfers between devices, send(): return lax.ppermute(value, AXES, pairs)  213 us
    all_gather x1, waiting for transfers between devices, per_device(): weights = lax.all_gather(shard, 'seq', axis=0)  113 us
    pallas_call x10, Pallas kernels, run_round(): pl.pallas_call(functools.partial(round_kernel, slot, with_latent), out_sh...  48.3 us
    ppermute x31, starting transfers between devices, send(): return lax.ppermute(value, AXES, pairs)  30.7 us
    unnamed x21, local copies, waits for them, and re-layouts  10.7 us
  transfers between devices with their start and end apart: 32, of which 9 were waited for; matrix products, arithmetic and copies ran while one was open for 2% of the time, Pallas kernels for 0%

profile of v2, /device:TPU:111, one launch (start us, length us, event | category | flops | bytes accessed | tf_op | source)
XLA Modules:
  0.0 439.9 jit_solution(2929786988319752415)
XLA Ops:
  6.5 2.2 pad_maximum_fusion.2
  8.7 0.0 all-gather.3.cloned.1.call-update
  8.7 0.7 collective-permute-start.2
  9.5 0.7 collective-permute-start.3
  10.2 1.5 slice.26
  11.8 2.1 collective-permute-start.1
  13.8 3.2 collective-permute-start
  17.1 0.4 pad_maximum_fusion.1
  17.5 2.0 slice_bitcast_fusion
  19.5 38.9 %collective-permute-done.1 = bf16[2,256,1536]{2,1,0:T(8,128)(2,1)S(1)} collective-permute-done((bf16[2,256,1536]{2,1,0:T(8,128)(2,1)S(1)}, bf16[2,256,1536]{2,1,0:T(8,128)(2,1)S(1)}, u32[]{:S(2)}, u32[]{:S(2)}) %collective-permute-start.1) | collective-permute-done | bytes 1572896 | tf_op jit(solution)/shard_map/ppermute | solution.py:193
  58.4 0.2 pad_bitcast_fusion
  58.5 2.8 collective-permute-done
  61.3 0.2 pad_bitcast_fusion.1
  61.5 0.8 pad_maximum_fusion
  62.3 2.6 fusion
  64.9 112.9 %all-gather.3.cloned.1.call-done = bf16[128,48,1536]{2,1,0:T(8,128)(2,1)} async-done(((bf16[4,48,1536]{2,1,0:T(8,128)(2,1)}), bf16[128,48,1536]{2,1,0:T(8,128)(2,1)}) %all-gather.3.cloned.1.call-update) | async-done | bytes 18874384 | tf_op jit(solution)/shard_map/all_gather | solution.py:197
  177.9 0.1 broadcast_in_dim.8.result_in
  178.0 6.4 %copy-done = bf16[128,48,1536]{2,1,0:T(8,128)(2,1)S(1)} copy-done((bf16[128,48,1536]{2,1,0:T(8,128)(2,1)S(1)}, bf16[128,48,1536]{2,1,0:T(8,128)(2,1)}, u32[]{:S(2)}) %copy-start) | copy-done | bytes 18874392
  184.4 2.0 copy-done.1
  186.4 1.3 copy-done.4
  187.6 0.6 round.10
  188.3 0.7 collective-permute-start.6
  189.0 0.7 collective-permute-start.5
  189.7 0.7 collective-permute-start.4
  190.4 5.9 %round.11 = (bf16[128,1536]{1,0:T(8,128)(2,1)S(1)}, bf16[18,64,1536]{2,1,0:T(8,128)(2,1)S(1)}, bf16[18,64,1536]{2,1,0:T(8,128)(2,1)S(1)}, bf16[3,128,1536]{2,1,0:T(8,128)(2,1)S(1)}) custom-call(s32[6,6]{1,0:T(8,128)S(1)} %copy-done.5, f32[1,128]{1,0:T(1,128)S(1)} %copy-done.6, ...), custom_call_target="tpu_custom_call", output_to_operand_aliasing={{1}: (7, {}), {2}: (8, {}), {3}: (9, {})} | custom-call | tf_op jit(solution)/shard_map/round/pallas_call | solution.py:148
  196.3 0.7 collective-permute-start.9
  197.0 0.7 collective-permute-start.8
  197.7 0.7 collective-permute-start.7
  198.4 0.6 round.12
  199.1 0.7 collective-permute-start.12
  199.8 0.7 collective-permute-start.11
  200.5 0.7 collective-permute-start.10
  201.2 0.9 round.13
  202.1 0.7 collective-permute-start.15
  202.8 0.7 collective-permute-start.14
  203.5 0.7 collective-permute-start.13
  204.2 3.1 round.14
  207.3 0.7 collective-permute-start.18
  208.0 0.7 collective-permute-start.17
  208.7 0.7 collective-permute-start.16
  209.4 2.8 round.15
  212.2 0.7 collective-permute-start.21
  212.9 0.7 collective-permute-start.20
  213.6 0.7 collective-permute-start.19
  214.3 2.8 round.16
  217.1 1.3 collective-permute-start.24
  218.4 1.3 collective-permute-start.23
  219.7 1.3 collective-permute-start.22
  221.0 142.0 %collective-permute-done.24.ahead_ref = bf16[128,1536]{1,0:T(8,128)(2,1)S(1)} collective-permute-done((bf16[128,1536]{1,0:T(8,128)(2,1)S(1)}, bf16[128,1536]{1,0:T(8,128)(2,1)S(1)}, u32[]{:S(2)}, u32[]{:S(2)}) %collective-permute-start.24) | collective-permute-done | bytes 393248 | tf_op jit(solution)/shard_map/ppermute | solution.py:193
  363.0 3.3 collective-permute-done.23.behind_ref
  366.3 10.2 %round.17 = (bf16[128,1536]{1,0:T(8,128)(2,1)S(1)}, bf16[18,64,1536]{2,1,0:T(8,128)(2,1)S(1)}, bf16[18,64,1536]{2,1,0:T(8,128)(2,1)S(1)}, bf16[3,128,1536]{2,1,0:T(8,128)(2,1)S(1)}) custom-call(s32[6,6]{1,0:T(8,128)S(1)} %copy-done.5, f32[1,128]{1,0:T(1,128)S(1)} %copy-done.6, ...), custom_call_target="tpu_custom_call", output_to_operand_aliasing={{1}: (7, {}), {2}: (8, {}), {3}: (9, {})} | custom-call | tf_op jit(solution)/shard_map/round/pallas_call | solution.py:148
  376.5 1.3 collective-permute-start.27
  377.8 1.3 collective-permute-start.26
  379.1 1.3 collective-permute-start.25
  380.4 5.4 %collective-permute-done.27.ahead_ref = bf16[128,1536]{1,0:T(8,128)(2,1)S(1)} collective-permute-done((bf16[128,1536]{1,0:T(8,128)(2,1)S(1)}, bf16[128,1536]{1,0:T(8,128)(2,1)S(1)}, u32[]{:S(2)}, u32[]{:S(2)}) %collective-permute-start.27) | collective-permute-done | bytes 393248 | tf_op jit(solution)/shard_map/ppermute | solution.py:193
  385.8 6.0 %collective-permute-done.26.behind_ref = bf16[128,1536]{1,0:T(8,128)(2,1)S(1)} collective-permute-done((bf16[128,1536]{1,0:T(8,128)(2,1)S(1)}, bf16[128,1536]{1,0:T(8,128)(2,1)S(1)}, u32[]{:S(2)}, u32[]{:S(2)}) %collective-permute-start.26) | collective-permute-done | bytes 393248 | tf_op jit(solution)/shard_map/ppermute | solution.py:193
  391.8 10.3 %round.18 = (bf16[128,1536]{1,0:T(8,128)(2,1)S(1)}, bf16[18,64,1536]{2,1,0:T(8,128)(2,1)S(1)}, bf16[18,64,1536]{2,1,0:T(8,128)(2,1)S(1)}, bf16[3,128,1536]{2,1,0:T(8,128)(2,1)S(1)}) custom-call(s32[6,6]{1,0:T(8,128)S(1)} %copy-done.5, f32[1,128]{1,0:T(1,128)S(1)} %copy-done.6, ...), custom_call_target="tpu_custom_call", output_to_operand_aliasing={{1}: (7, {}), {2}: (8, {}), {3}: (9, {})} | custom-call | tf_op jit(solution)/shard_map/round/pallas_call | solution.py:148
  402.1 1.3 collective-permute-start.30
  403.4 1.3 collective-permute-start.29
  404.7 1.3 collective-permute-start.28
  406.0 11.2 %collective-permute-done.30.ahead_ref = bf16[128,1536]{1,0:T(8,128)(2,1)S(1)} collective-permute-done((bf16[128,1536]{1,0:T(8,128)(2,1)S(1)}, bf16[128,1536]{1,0:T(8,128)(2,1)S(1)}, u32[]{:S(2)}, u32[]{:S(2)}) %collective-permute-start.30) | collective-permute-done | bytes 393248 | tf_op jit(solution)/shard_map/ppermute | solution.py:193
  417.2 3.2 collective-permute-done.29.behind_ref
  420.4 11.1 %round.19 = (bf16[128,1536]{1,0:T(8,128)(2,1)}, bf16[18,64,1536]{2,1,0:T(8,128)(2,1)S(1)}, bf16[18,64,1536]{2,1,0:T(8,128)(2,1)S(1)}, bf16[3,128,1536]{2,1,0:T(8,128)(2,1)S(1)}) custom-call(s32[6,6]{1,0:T(8,128)S(1)} %copy-done.5, f32[1,128]{1,0:T(1,128)S(1)} %copy-done.6, ...), custom_call_target="tpu_custom_call", output_to_operand_aliasing={{1}: (7, {}), {2}: (8, {}), {3}: (9, {})} | custom-call | tf_op jit(solution)/shard_map/round/pallas_call | solution.py:148
  431.5 1.0 copy.70
  (42 shorter events, 0.1 us)
Async XLA Ops:
  6.5 10.5 %copy-start.9 = (bf16[384,1536]{1,0:T(8,128)(2,1)S(1)}, bf16[384,1536]{1,0:T(8,128)(2,1)}, u32[]{:S(2)}) copy-start(bf16[384,1536]{1,0:T(8,128)(2,1)} %param.9) | copy-start | bytes 3538948
  6.5 171.3 %all-gather.3.cloned.1.call-start = ((), (), s32[]{:S(2)}) async-start(), calls=%async_computation | async-start | bytes 19464192 | tf_op jit(solution)/shard_map/all_gather | solution.py:197
  8.7 8.3 %collective-permute-start.2 = (bf16[384,1536]{1,0:T(8,128)(2,1)}, bf16[384,1536]{1,0:T(8,128)(2,1)S(1)}, u32[]{:S(2)}, u32[]{:S(2)}) collective-permute-start(bf16[384,1536]{1,0:T(8,128)(2,1)} %param.9), channel_id=1, source_target_pairs={{0,1},{1,2},{2,3},{3,4},{4,5},{5,6},{6,7},{7,8},{8,9},{9,10},{10,1... | collective-permute-start | bytes 3538952 | tf_op jit(solution)/shard_map/ppermute | solution.py:193
  9.5 7.6 %collective-permute-start.3 = (bf16[384,1536]{1,0:T(8,128)(2,1)}, bf16[384,1536]{1,0:T(8,128)(2,1)S(1)}, u32[]{:S(2)}, u32[]{:S(2)}) collective-permute-start(bf16[384,1536]{1,0:T(8,128)(2,1)} %param.9), channel_id=1, source_target_pairs={{1,0},{2,1},{3,2},{4,3},{5,4},{6,5},{7,6},{8,7},{9,8},{10,9},{11,1... | collective-permute-start | bytes 3538952 | tf_op jit(solution)/shard_map/ppermute | solution.py:193
  11.8 46.6 %collective-permute-start.1 = (bf16[2,256,1536]{2,1,0:T(8,128)(2,1)S(1)}, bf16[2,256,1536]{2,1,0:T(8,128)(2,1)S(1)}, u32[]{:S(2)}, u32[]{:S(2)}) collective-permute-start(bf16[2,256,1536]{2,1,0:T(8,128)(2,1)S(1)} %slice.26), channel_id=1, source_target_pairs={{1,0},{2,1},{3,2},{4,3},{5,4},{6,5},{7,6},{8,7},{9,8},{10,9},{11,1... | collective-permute-start | bytes 4718600 | tf_op jit(solution)/shard_map/ppermute | solution.py:193
  13.8 47.5 %collective-permute-start = (bf16[2,256,1536]{2,1,0:T(8,128)(2,1)S(1)}, bf16[2,256,1536]{2,1,0:T(8,128)(2,1)S(1)}, u32[]{:S(2)}, u32[]{:S(2)}) collective-permute-start(bf16[2,256,1536]{2,1,0:T(8,128)(2,1)S(1)} %slice.26), channel_id=1, source_target_pairs={{0,1},{1,2},{2,3},{3,4},{4,5},{5,6},{6,7},{7,8},{8,9},{9,10},{10,1... | collective-permute-start | bytes 4718600 | tf_op jit(solution)/shard_map/ppermute | solution.py:193
  19.5 42.0 %copy-start.8 = (bf16[1,2,384,1536]{3,2,1,0:T(8,128)(2,1)S(1)}, bf16[1,2,384,1536]{3,2,1,0:T(8,128)(2,1)}, u32[]{:S(2)}) copy-start(bf16[1,2,384,1536]{3,2,1,0:T(8,128)(2,1)} %param.10) | copy-start | bytes 7077892
  62.3 115.7 %copy-start.5 = (s32[6,6]{1,0:T(8,128)S(1)}, s32[6,6]{1,0:T(8,128)}, u32[]{:S(2)}) copy-start(s32[6,6]{1,0:T(8,128)} %mask_ref.19) | copy-start | bytes 436
  62.3 115.7 %copy-start.6 = (f32[1,128]{1,0:T(1,128)S(1)}, f32[1,128]{1,0:T(1,128)}, u32[]{:S(2)}) copy-start(f32[1,128]{1,0:T(1,128)} %gain_q_ref.19) | copy-start | bytes 1540
  62.3 115.7 %copy-start.7 = (f32[1,128]{1,0:T(1,128)S(1)}, f32[1,128]{1,0:T(1,128)}, u32[]{:S(2)}) copy-start(f32[1,128]{1,0:T(1,128)} %gain_k_ref.19) | copy-start | bytes 1540
  178.0 6.4 %copy-start = (bf16[128,48,1536]{2,1,0:T(8,128)(2,1)S(1)}, bf16[128,48,1536]{2,1,0:T(8,128)(2,1)}, u32[]{:S(2)}) copy-start(bf16[128,48,1536]{2,1,0:T(8,128)(2,1)} %all-gather.3.cloned.1.call-done) | copy-start | bytes 56623108
  184.4 2.0 copy-start.1
  186.4 1.3 copy-start.4
  187.6 2.7 copy-start.3
  188.3 2.1 collective-permute-start.6
  189.0 1.4 collective-permute-start.5
  189.7 0.7 collective-permute-start.4
  190.4 8.1 %copy-start.2 = (bf16[3,128,1536]{2,1,0:T(8,128)(2,1)S(1)}, bf16[3,128,1536]{2,1,0:T(8,128)(2,1)}, u32[]{:S(2)}) copy-start(bf16[3,128,1536]{2,1,0:T(8,128)(2,1)} %get-tuple-element.81.rest_0_) | copy-start | bytes 3538948
  196.3 2.1 collective-permute-start.9
  197.0 1.4 collective-permute-start.8
  197.7 0.7 collective-permute-start.7
  199.1 2.1 collective-permute-start.12
  199.8 1.4 collective-permute-start.11
  200.5 0.7 collective-permute-start.10
  202.1 2.1 collective-permute-start.15
  202.8 1.4 collective-permute-start.14
  203.5 0.7 collective-permute-start.13
  207.3 2.1 collective-permute-start.18
  208.0 1.4 collective-permute-start.17
  208.7 0.7 collective-permute-start.16
  212.2 2.1 collective-permute-start.21
  212.9 1.4 collective-permute-start.20
  213.6 0.7 collective-permute-start.19
  217.1 145.9 %collective-permute-start.24 = (bf16[128,1536]{1,0:T(8,128)(2,1)S(1)}, bf16[128,1536]{1,0:T(8,128)(2,1)S(1)}, u32[]{:S(2)}, u32[]{:S(2)}) collective-permute-start(bf16[128,1536]{1,0:T(8,128)(2,1)S(1)} %get-tuple-element.66), channel_id=1, source_target_pairs={{129,160},{130,161},{131,162},{132,163},{133,164},{134,165},{135,1... | collective-permute-start | bytes 1179656 | tf_op jit(solution)/shard_map/ppermute | solution.py:193
  218.4 147.9 %collective-permute-start.23 = (bf16[128,1536]{1,0:T(8,128)(2,1)S(1)}, bf16[128,1536]{1,0:T(8,128)(2,1)S(1)}, u32[]{:S(2)}, u32[]{:S(2)}) collective-permute-start(bf16[128,1536]{1,0:T(8,128)(2,1)S(1)} %get-tuple-element.66), channel_id=1, source_target_pairs={{128,161},{129,162},{130,163},{131,164},{132,165},{133,166},{134,1... | collective-permute-start | bytes 1179656 | tf_op jit(solution)/shard_map/ppermute | solution.py:193
  219.7 146.6 %collective-permute-start.22 = (bf16[128,1536]{1,0:T(8,128)(2,1)S(1)}, bf16[128,1536]{1,0:T(8,128)(2,1)S(1)}, u32[]{:S(2)}, u32[]{:S(2)}) collective-permute-start(bf16[128,1536]{1,0:T(8,128)(2,1)S(1)} %get-tuple-element.66), channel_id=1, source_target_pairs={{128,160},{129,161},{130,162},{131,163},{132,164},{133,165},{134,1... | collective-permute-start | bytes 1179656 | tf_op jit(solution)/shard_map/ppermute | solution.py:193
  376.5 9.3 %collective-permute-start.27 = (bf16[128,1536]{1,0:T(8,128)(2,1)S(1)}, bf16[128,1536]{1,0:T(8,128)(2,1)S(1)}, u32[]{:S(2)}, u32[]{:S(2)}) collective-permute-start(bf16[128,1536]{1,0:T(8,128)(2,1)S(1)} %get-tuple-element.70), channel_id=1, source_target_pairs={{161,192},{162,193},{163,194},{164,195},{165,196},{166,197},{167,1... | collective-permute-start | bytes 1179656 | tf_op jit(solution)/shard_map/ppermute | solution.py:193
  377.8 14.0 %collective-permute-start.26 = (bf16[128,1536]{1,0:T(8,128)(2,1)S(1)}, bf16[128,1536]{1,0:T(8,128)(2,1)S(1)}, u32[]{:S(2)}, u32[]{:S(2)}) collective-permute-start(bf16[128,1536]{1,0:T(8,128)(2,1)S(1)} %get-tuple-element.70), channel_id=1, source_target_pairs={{160,193},{161,194},{162,195},{163,196},{164,197},{165,198},{166,1... | collective-permute-start | bytes 1179656 | tf_op jit(solution)/shard_map/ppermute | solution.py:193
  379.1 12.7 %collective-permute-start.25 = (bf16[128,1536]{1,0:T(8,128)(2,1)S(1)}, bf16[128,1536]{1,0:T(8,128)(2,1)S(1)}, u32[]{:S(2)}, u32[]{:S(2)}) collective-permute-start(bf16[128,1536]{1,0:T(8,128)(2,1)S(1)} %get-tuple-element.70), channel_id=1, source_target_pairs={{160,192},{161,193},{162,194},{163,195},{164,196},{165,197},{166,1... | collective-permute-start | bytes 1179656 | tf_op jit(solution)/shard_map/ppermute | solution.py:193
  402.1 15.1 %collective-permute-start.30 = (bf16[128,1536]{1,0:T(8,128)(2,1)S(1)}, bf16[128,1536]{1,0:T(8,128)(2,1)S(1)}, u32[]{:S(2)}, u32[]{:S(2)}) collective-permute-start(bf16[128,1536]{1,0:T(8,128)(2,1)S(1)} %get-tuple-element.74), channel_id=1, source_target_pairs={{193,224},{194,225},{195,226},{196,227},{197,228},{198,229},{199,2... | collective-permute-start | bytes 1179656 | tf_op jit(solution)/shard_map/ppermute | solution.py:193
  403.4 17.1 %collective-permute-start.29 = (bf16[128,1536]{1,0:T(8,128)(2,1)S(1)}, bf16[128,1536]{1,0:T(8,128)(2,1)S(1)}, u32[]{:S(2)}, u32[]{:S(2)}) collective-permute-start(bf16[128,1536]{1,0:T(8,128)(2,1)S(1)} %get-tuple-element.74), channel_id=1, source_target_pairs={{192,225},{193,226},{194,227},{195,228},{196,229},{197,230},{198,2... | collective-permute-start | bytes 1179656 | tf_op jit(solution)/shard_map/ppermute | solution.py:193
  404.7 15.8 %collective-permute-start.28 = (bf16[128,1536]{1,0:T(8,128)(2,1)S(1)}, bf16[128,1536]{1,0:T(8,128)(2,1)S(1)}, u32[]{:S(2)}, u32[]{:S(2)}) collective-permute-start(bf16[128,1536]{1,0:T(8,128)(2,1)S(1)} %get-tuple-element.74), channel_id=1, source_target_pairs={{192,224},{193,225},{194,226},{195,227},{196,228},{197,229},{198,2... | collective-permute-start | bytes 1179656 | tf_op jit(solution)/shard_map/ppermute | solution.py:193
Sparse Core Ops, SparseCore 0:
  9.9 167.8 all-gather.2
